TPU v7x, 256 devices: a whole 4x4x8 slice. The times are simulated.
256 devices in a mesh: rows: 8 (over z_hi, x), lat: 32 (over y, z_lo, core).
Axes of the slice: x: 4, y: 4, z: 8 (z_hi: 2, z_lo: 4; z = z_hi * 4 + z_lo), core: 2. Of those that a mesh axis runs over, the one named last changes fastest.
Arguments:
- residual: bfloat16 [1024, 4608], P('rows', 'lat'), may hold values from -64 to 64
- enc_weight: bfloat16 [4608, 65536], P('rows', 'lat'), may hold values from -0.09375 to 0.09375
- dec_weight: bfloat16 [65536, 4608], P('lat', 'rows'), may hold values from -0.078125 to 0.078125
- enc_bias: float32 [65536], P('lat'), may hold values from -3 to 3
- dec_bias: float32 [4608], P('rows'), may hold values from -3 to 3
- active_blocks: int32 [8, 96], replicated, may hold values from 0 to 511, as said below
- active_counts: int32 [1024], P('rows'), may hold values from 1 to 96, as said below
Outputs:
- latents: bfloat16 [1024, 65536], P('rows', 'lat')
- recon: bfloat16 [1024, 4608], P('lat', 'rows')
Inputs may be any that keep to these rules, and one draw needn't show every extreme that they name: `active_blocks`: each row lists 96 different latent blocks; at most 6 of them lie among the 16 blocks of one index of lat, and exactly 6 for some index in every row. `active_counts`: in every row block some row uses all 96 entries and some row uses one.
All inputs are finite; a program needn't handle non-finite values.
Results may differ from a plain program's by a relative error of at most 0.0058.
Values may be sent and summed in bfloat16 or wider, within the bound.
No kernel may reach another device: no remote copies, remote signals or barrier semaphores. Data moves between devices by JAX's collectives and lax.ppermute only.
A program may use at most 128 MiB of HBM per device.

v0:
```python
import functools

import jax
import jax.numpy as jnp
from jax import lax
from jax.experimental import pallas as pl
from jax.experimental.pallas import tpu as pltpu
from jax.sharding import Mesh
from jax.sharding import PartitionSpec as P


BLOCK = 128
CAP = 6
TOKENS = 1024
D = 4608
SHARD_BLOCKS = 16
ACTIVE = 96
SLICE = 576
SUB = 32
ROWS = ("zh", "x")
LAT = ("y", "zl", "c")
SIZES = {"zh": 2, "x": 4, "y": 4, "zl": 4, "c": 2}
BF16 = jnp.bfloat16
F32 = jnp.float32

VMEM = pl.BlockSpec(memory_space=pltpu.VMEM)
SMEM = pl.BlockSpec(memory_space=pltpu.SMEM)
ANY = pl.BlockSpec(memory_space=pl.ANY)


def swap(value, axis, k):
    return lax.ppermute(value, axis, [(i, i ^ k) for i in range(SIZES[axis])])


def gather4(value, axis):
    far, near, last = (swap(value, axis, k) for k in (2, 1, 3))
    return jnp.concatenate([value, near, far, last], axis=0)


def call(kernel, outs, operands, specs, flops=0, size=0, scratch=()):
    return pl.pallas_call(
        kernel,
        out_shape=outs,
        in_specs=specs,
        out_specs=jax.tree.map(lambda _: VMEM, outs),
        scratch_shapes=scratch,
        compiler_params=pltpu.CompilerParams(vmem_limit_bytes=GRANT),
        cost_estimate=pl.CostEstimate(flops=flops, bytes_accessed=size, transcendentals=0),
    )(*operands)


def bits(pos):
    return pos[0], pos[1], pos[2], pos[3], pos[4]


GRANT = 10 * 2**20
WIDE = TOKENS + BLOCK


def row_group(zh, y, zl, c):
    return (y * 4 + (zl ^ (3 * zh))) * 2 + c


def on_diagonal(group):
    shape = (SUB, TOKENS)
    row = lax.broadcasted_iota(jnp.int32, shape, 0)
    return lax.broadcasted_iota(jnp.int32, shape, 1) == row + group * SUB


def split3(value):
    high = value.astype(BF16).astype(F32)
    mid = (value - high).astype(BF16).astype(F32)
    return high, mid, (value - high - mid).astype(BF16).astype(F32)


def pack(counts, diagonal, energy):
    row = lax.broadcasted_iota(jnp.int32, (SUB, BLOCK), 0)
    extra = jnp.where(row < 8, counts, 0.0)
    for i, part in enumerate(split3(diagonal) + split3(energy)):
        extra = jnp.where(row == 8 + i, part, extra)
    return extra


def gram_kernel(pos, near, other, counts, wide, narrow, full, own):
    zh, x, y, zl, c = bits(pos)
    for jc, half in enumerate((near, other)):
        for jy in range(4):
            for jz in range(4):
                zs = zl ^ jz
                feature = pl.multiple_of(((zs & 1) * 2 + (c ^ jc)) * 144, 16)
                source = ((zs // 2) ^ (x & 1) ^ zh) * 4 + ((zh * 2 + x // 2 + x + 2 - (y ^ jy)) & 3)
                row = pl.multiple_of(source * BLOCK, BLOCK)
                full[pl.ds(feature, 144), pl.ds(row, BLOCK)] = half[jy * 4 + jz]
    group = row_group(zh, y, zl, c)
    rows = full[:, pl.ds(pl.multiple_of(group // 4 * BLOCK, BLOCK), BLOCK)].astype(F32).T.astype(BF16)
    mine = rows[0:SUB]
    for g in range(1, 4):
        mine = jnp.where(group % 4 == g, rows[g * SUB : (g + 1) * SUB], mine)
    own[...] = mine
    g = jnp.dot(mine, full[...], preferred_element_type=F32)
    mask = on_diagonal(group)
    diagonal = jnp.sum(jnp.where(mask, g, 0.0), axis=0, keepdims=True)
    diagonal = sum(diagonal[:, i * BLOCK : (i + 1) * BLOCK] for i in range(TOKENS // BLOCK))
    g = jnp.where(mask, 0.0, g)
    wide[:, :TOKENS] = g
    narrow[:, :TOKENS] = g.astype(BF16)
    spread = full[...].astype(F32)
    total = jnp.sum(jnp.sum(spread * spread, axis=0, keepdims=True), axis=1, keepdims=True)
    shape = (SUB, BLOCK)
    row = lax.broadcasted_iota(jnp.int32, shape, 0)
    spot = jnp.where(row == zh * 4 + x, jnp.broadcast_to(counts[...], shape), 0.0)
    extra = pack(spot, jnp.broadcast_to(diagonal, shape), jnp.broadcast_to(total, shape))
    wide[:, TOKENS:] = extra
    narrow[:, TOKENS:] = extra.astype(BF16)


def unpack(extra):
    return extra[8:9] + extra[9:10] + extra[10:11], extra[11:12] + extra[12:13] + extra[13:14]


def gram_sum_kernel(mine, by1, by2, by3, wide, narrow):
    g = mine[...] + by1[...].astype(F32) + by2[...].astype(F32) + by3[...].astype(F32)
    wide[...] = g
    narrow[:, :TOKENS] = g[:, :TOKENS].astype(BF16)
    extra = g[:, TOKENS:]
    shape = (SUB, BLOCK)
    diagonal, energy = (jnp.broadcast_to(v, shape) for v in unpack(extra))
    narrow[:, TOKENS:] = pack(extra, diagonal, energy).astype(BF16)


def white_kernel(pos, mine, theirs, full, own, out):
    zh, _, y, zl, c = bits(pos)
    g = mine[...] + theirs[...].astype(F32)
    diagonal, energy = unpack(g[:, TOKENS:])
    mean_sq = energy[:, 0:1] / (TOKENS * D)
    diagonal = jnp.broadcast_to(jnp.concatenate([diagonal] * (TOKENS // BLOCK), axis=1), (SUB, TOKENS))
    g = jnp.where(on_diagonal(row_group(zh, y, zl, c)), diagonal, g[:, :TOKENS])
    chat = g / (TOKENS * (mean_sq + 1e-05))
    high = chat.astype(BF16)
    low = (chat - high.astype(F32)).astype(BF16)
    both = jnp.concatenate([high, low], axis=0)
    term = lax.dot_general(both, full[...], (((1,), (1,)), ((), ())), preferred_element_type=F32)
    out[0] = (1.5 * own[...].astype(F32) - 0.5 * (term[:SUB] + term[SUB:])).astype(BF16)


def counts_kernel(pos, mine, theirs, out, tile):
    tile[...] = mine[0:8, TOKENS:] + theirs[0:16, TOKENS:].astype(F32)[0:8]
    for zb in range(2):
        row = tile[pl.ds(pos[1] + 4 * zb, 1), :]
        out[zb] = jnp.broadcast_to(row, (BLOCK, BLOCK)).T


def encode_kernel(p, pos, tab, after, near, other, weight, o0, o1, o2, o3):
    zh, x, y, zl, _ = bits(pos)
    for k, out in ((2, o2), (1, o1), (3, o3), (0, o0)):
        xb = x ^ k
        for zb in range(2):
            b = zb * 4 + xb
            jy = y ^ (zb * 2 + xb // 2)
            places = [jy * 4 + (zl ^ (3 * zh) ^ ((xb & 1) * 2 + q)) for q in range(2)]
            rows = jnp.concatenate([half[place] for half in (near, other) for place in places], axis=0)
            cols = [weight[:, pl.ds(pl.multiple_of(tab[b, 2 * p + e] * BLOCK, BLOCK), BLOCK)] for e in range(2)]
            part = jnp.dot(rows, jnp.concatenate(cols, axis=1), preferred_element_type=F32)
            out[zb] = part.astype(BF16)


def sum_kernel(after, p0, p1, p2, p3, wide, narrow):
    total = p0[...].astype(F32) + p1[...].astype(F32) + p2[...].astype(F32) + p3[...].astype(F32)
    wide[...] = total
    narrow[...] = total.astype(BF16)


def row_start(q, jc, c):
    return pl.multiple_of(q * 64 + (c ^ jc) * SUB, SUB)


def latent_kernel(p, pos, tab, after, mine, theirs, bias, counts, out):
    _, x, _, _, c = bits(pos)
    for zb in range(2):
        b = zb * 4 + x
        limits = jnp.concatenate(
            [counts[zb, pl.ds(row_start(q, jc, c), SUB), :] for jc in range(2) for q in range(2)], axis=0
        )
        for e in range(2):
            slot = 2 * p + e
            cols = slice(e * BLOCK, (e + 1) * BLOCK)
            pre = mine[zb, :, cols] + theirs[zb, :, cols].astype(F32) + bias[pl.ds(tab[b, slot], 1), :]
            rank = tab[b, 8 + slot].astype(F32)
            out[zb, :, cols] = jnp.where(rank < limits, jnp.maximum(pre, 0.0), 0.0).astype(BF16)


def spread_kernel(pos, tab, lat0, lat1, lat2, out):
    zh, x, _, _, c = bits(pos)
    out[...] = jnp.zeros_like(out)
    b = zh * 4 + x
    for slot in range(CAP):
        @pl.when(tab[b, 8 + slot] < ACTIVE)
        def _():
            start = pl.multiple_of(tab[b, slot] * BLOCK, BLOCK)
            lat = (lat0, lat1, lat2)[slot // 2]
            cols = slice(slot % 2 * BLOCK, (slot % 2 + 1) * BLOCK)
            for jc in range(2):
                for q in range(2):
                    piece = jc * 2 + q
                    out[pl.ds(row_start(q, jc, c), SUB), pl.ds(start, BLOCK)] = lat[
                        zh, piece * SUB : (piece + 1) * SUB, cols
                    ]


def decode_pair(p, tab, lat, zb, b, weight):
    tiles = [weight[:, pl.ds(pl.multiple_of(tab[b, 2 * p + e] * BLOCK, BLOCK), BLOCK)] for e in range(2)]
    return lax.dot_general(
        lat[zb], jnp.concatenate(tiles, axis=1), (((1,), (1,)), ((), ())), preferred_element_type=F32
    )


def decode_kernel(pos, tab, after, *refs):
    first, second, weight, out = refs[0:4], refs[4:8], refs[8], refs[9]
    x = pos[1]
    for k in range(4):
        for zb in range(2):
            b = zb * 4 + (x ^ k)
            out[k, zb] = decode_pair(0, tab, first[k], zb, b, weight) + decode_pair(1, tab, second[k], zb, b, weight)


def finish_kernel(pos, tab, total, l0, l1, l2, l3, weight, mine, theirs):
    _, x, _, _, _ = bits(pos)
    for k, lat in enumerate((l0, l1, l2, l3)):
        xb = x ^ k
        for zb in range(2):
            acc = total[k, zb] + decode_pair(2, tab, lat, zb, zb * 4 + xb, weight)
            ky = zb * 2 + xb // 2
            for q in range(2):
                kz = (xb & 1) * 2 + q
                mine[ky, kz] = acc[q * SUB : (q + 1) * SUB]
                theirs[ky, kz] = acc[64 + q * SUB : 64 + (q + 1) * SUB].astype(BF16)


def join_kernel(mine, theirs, out):
    out[...] = (mine[...] + theirs[...].astype(F32)).astype(BF16)


def total_kernel(parts, bias, out):
    total = parts[0].astype(F32)
    for i in range(1, 16):
        total = total + parts[i].astype(F32)
    out[...] = (total + bias[...]).astype(BF16)


def tables(active_blocks, lat_index):
    ids = lat_index * SHARD_BLOCKS + jnp.arange(SHARD_BLOCKS, dtype=jnp.int32)
    matches = active_blocks[:, :, None] == ids[None, None, :]
    places = jnp.arange(ACTIVE, dtype=jnp.int32)[None, :, None]
    rank = jnp.sum(jnp.where(matches, places, 0), axis=1)
    listed = jnp.any(matches, axis=1).astype(jnp.int32)
    block = jnp.arange(SHARD_BLOCKS, dtype=jnp.int32)
    before = (block[:, None] < block[None, :]).astype(jnp.int32)
    slot = jnp.sum(listed[:, :, None] * before[None], axis=1)
    chosen = (slot[:, :, None] == jnp.arange(8, dtype=jnp.int32)[None, None, :]) & (listed[:, :, None] > 0)
    index = jnp.sum(jnp.where(chosen, block[None, :, None], 0), axis=1)
    ranks = jnp.sum(jnp.where(chosen, rank[:, :, None] - ACTIVE, 0), axis=1) + ACTIVE
    return jnp.concatenate([index, ranks], axis=1)


def shards(residual, enc_weight, dec_weight, enc_bias, dec_bias, active_blocks, active_counts):
    zh, x, y, zl, c = (lax.axis_index(a) for a in ("zh", "x", "y", "zl", "c"))
    pos = jnp.stack([zh, x, y, zl, c]).astype(jnp.int32)
    tab = tables(active_blocks, (y * 4 + zl) * 2 + c)

    pairs = []
    for source in range(256):
        r, lat = divmod(source, 32)
        half, xs = divmod(r, 4)
        ys, zs, core = lat // 8, lat // 2 % 4, lat % 2
        zh_to, x_to = divmod(lat // 4, 4)
        y_to, z_to = (ys + x_to - xs + 2) % 4, zs ^ (2 * (zh_to ^ half))
        pairs.append((source, (lat // 4) * 32 + y_to * 8 + z_to * 2 + core))
    own = lax.ppermute(residual.T, ROWS + LAT, pairs)
    near = gather4(gather4(own[None], "zl"), "y")
    other = swap(near, "c", 1)

    counts = active_counts.astype(F32).reshape(1, BLOCK)
    wide, narrow, full, own = call(
        gram_kernel,
        (
            jax.ShapeDtypeStruct((SUB, WIDE), F32),
            jax.ShapeDtypeStruct((SUB, WIDE), BF16),
            jax.ShapeDtypeStruct((SLICE, TOKENS), BF16),
            jax.ShapeDtypeStruct((SUB, SLICE), BF16),
        ),
        (pos, near, other, counts),
        [SMEM, VMEM, VMEM, VMEM],
        flops=2 * SUB * TOKENS * SLICE,
        size=1500000,
    )
    by2, by1, by3 = (swap(narrow, "x", k) for k in (2, 1, 3))
    mine, narrow = call(
        gram_sum_kernel,
        (jax.ShapeDtypeStruct((SUB, WIDE), F32), jax.ShapeDtypeStruct((SUB, WIDE), BF16)),
        (wide, by1, by2, by3),
        [VMEM] * 4,
        size=600000,
    )
    theirs = lax.ppermute(narrow, ("zh", "zl"), [(i, 7 - i) for i in range(8)])
    white = call(
        white_kernel,
        jax.ShapeDtypeStruct((1, SUB, SLICE), BF16),
        (pos, mine, theirs, full, own),
        [SMEM] + [VMEM] * 4,
        flops=4 * SUB * TOKENS * SLICE,
        size=1500000,
    )
    counts = call(
        counts_kernel,
        jax.ShapeDtypeStruct((2, BLOCK, BLOCK), F32),
        (pos, mine, theirs),
        [SMEM, VMEM, VMEM],
        size=500000,
        scratch=[pltpu.VMEM((8, BLOCK), F32)],
    )

    white_near = gather4(gather4(white, "zl"), "y")
    white_other = swap(white_near, "c", 1)
    bias = enc_bias.reshape(SHARD_BLOCKS, BLOCK)
    piece = jax.ShapeDtypeStruct((2, BLOCK, 2 * BLOCK), BF16)
    chunks = range(CAP // 2)
    sent, sums, lats = [], [], []
    for p in chunks:
        sent.append(
            call(
                functools.partial(encode_kernel, p),
                (piece,) * 4,
                (pos, tab, sent[-1][0] if p else white_near, white_near, white_other, enc_weight),
                [SMEM, SMEM, ANY, VMEM, VMEM, VMEM],
                flops=TOKENS * SLICE * 4 * BLOCK,
                size=3000000,
            )
        )
    arrived = [[swap(sent[p][k], "x", k) for k in (2, 1, 3)] for p in chunks]
    for p in chunks:
        sums.append(
            call(
                sum_kernel,
                (jax.ShapeDtypeStruct(piece.shape, F32), piece),
                (sums[-1][1] if p else sent[-1][0], sent[p][0], *arrived[p]),
                [ANY] + [VMEM] * 4,
                size=900000,
            )
        )
    theirs = [swap(sums[p][1], "zh", 1) for p in chunks]
    for p in chunks:
        lats.append(
            call(
                functools.partial(latent_kernel, p),
                piece,
                (pos, tab, lats[-1] if p else white_near, sums[p][0], theirs[p], bias, counts),
                [SMEM, SMEM, ANY, VMEM, VMEM, VMEM, VMEM],
                size=700000,
            )
        )
    arrived = []
    for p in chunks:
        by2, by1, by3 = (swap(lats[p], "x", k) for k in (2, 1, 3))
        arrived.append((lats[p], by1, by2, by3))
    dec_weight = dec_weight.T
    total = call(
        decode_kernel,
        jax.ShapeDtypeStruct((4, 2, BLOCK, SLICE), F32),
        (pos, tab, lats[-1], *arrived[0], *arrived[1], dec_weight),
        [SMEM, SMEM, ANY] + [VMEM] * 9,
        flops=TOKENS * SLICE * 8 * BLOCK,
        size=5000000,
    )
    part = (4, 4, SUB, SLICE)
    mine, theirs = call(
        finish_kernel,
        (jax.ShapeDtypeStruct(part, F32), jax.ShapeDtypeStruct(part, BF16)),
        (pos, tab, total, *arrived[2], dec_weight),
        [SMEM, SMEM] + [VMEM] * 6,
        flops=TOKENS * SLICE * 4 * BLOCK,
        size=5000000,
    )
    latents = call(
        spread_kernel,
        jax.ShapeDtypeStruct((BLOCK, SHARD_BLOCKS * BLOCK), BF16),
        (pos, tab, *lats),
        [SMEM, SMEM] + [VMEM] * 3,
        size=1000000,
    )
    joined = call(
        join_kernel, jax.ShapeDtypeStruct(part, BF16), (mine, swap(theirs, "c", 1)), [VMEM] * 2, size=4000000
    ).reshape(16, SUB, SLICE)
    recon = call(
        total_kernel,
        jax.ShapeDtypeStruct((SUB, SLICE), BF16),
        (lax.all_to_all(joined, ("y", "zl"), 0, 0, tiled=True), dec_bias.reshape(1, SLICE)),
        [VMEM] * 2,
        size=600000,
    )
    return latents, recon


def solution(mesh):
    fine = Mesh(mesh.devices.reshape(tuple(SIZES.values())), tuple(SIZES))
    in_specs = (P(ROWS, LAT), P(ROWS, LAT), P(LAT, ROWS), P(LAT), P(ROWS), P(), P(ROWS))
    out_specs = (P(ROWS, LAT), P(LAT, ROWS))
    return jax.shard_map(shards, mesh=fine, in_specs=in_specs, out_specs=out_specs, check_vma=False)
```

profile of v0, /device:TPU:2, one launch (start us, length us, event | category | flops | bytes accessed | tf_op | source)
XLA Modules:
  0.0 158.5 jit_solution(8684867911026195033)
XLA Ops:
  2.3 8.5 %collective-permute-done = bf16[144,128]{1,0:T(8,128)(2,1)S(1)} collective-permute-done((bf16[144,128]{1,0:T(8,128)(2,1)}, bf16[144,128]{1,0:T(8,128)(2,1)S(1)}, u32[]{:S(2)}, u32[]{:S(2)}) %collective-permute-start) | collective-permute-done | bytes 36896 | tf_op jit(solution)/shard_map/ppermute | solution.py:278
  11.7 3.4 %collective-permute-start.3 = (bf16[1,144,128]{2,1,0:T(8,128)(2,1)S(1)}, bf16[1,144,128]{2,1,0:T(8,128)(2,1)S(1)}, u32[]{:S(2)}, u32[]{:S(2)}) collective-permute-start(bf16[1,144,128]{2,1,0:T(8,128)(2,1)S(1)} %bitcast.20), channel_id=1, source_target_pairs={{0,6},{2,4},{4,2},{6,0},{1,7},{3,5},{5,3},{7,1},{8,14},{10,12},{12... | collective-permute-start | bytes 110600 | tf_op jit(solution)/shard_map/ppermute | solution.py:32
  18.7 4.7 %collective-permute-start.5 = (bf16[4,144,128]{2,1,0:T(8,128)(2,1)S(1)}, bf16[4,144,128]{2,1,0:T(8,128)(2,1)S(1)}, u32[]{:S(2)}, u32[]{:S(2)}) collective-permute-start(bf16[4,144,128]{2,1,0:T(8,128)(2,1)S(1)} %pad_maximum_fusion.1), channel_id=1, source_target_pairs={{0,16},{8,24},{16,0},{24,8},{1,17},{9,25},{17,1},{25,9},{2,18},{10... | collective-permute-start | bytes 442376 | tf_op jit(solution)/shard_map/ppermute | solution.py:32
  24.1 4.0 %collective-permute-done.5 = bf16[4,144,128]{2,1,0:T(8,128)(2,1)S(1)} collective-permute-done((bf16[4,144,128]{2,1,0:T(8,128)(2,1)S(1)}, bf16[4,144,128]{2,1,0:T(8,128)(2,1)S(1)}, u32[]{:S(2)}, u32[]{:S(2)}) %collective-permute-start.5) | collective-permute-done | bytes 147488 | tf_op jit(solution)/shard_map/ppermute | solution.py:32
  33.1 3.2 %collective-permute-start.10 = (bf16[32,1152]{1,0:T(8,128)(2,1)S(1)}, bf16[32,1152]{1,0:T(8,128)(2,1)S(1)}, u32[]{:S(2)}, u32[]{:S(2)}) collective-permute-start(bf16[32,1152]{1,0:T(8,128)(2,1)S(1)} %get-tuple-element.29), channel_id=1, source_target_pairs={{0,96},{32,64},{64,32},{96,0},{1,97},{33,65},{65,33},{97,1},{2,98}... | collective-permute-start | bytes 221192 | tf_op jit(solution)/shard_map/ppermute | solution.py:32
  37.3 2.0 %collective-permute-start.9 = (bf16[32,1152]{1,0:T(8,128)(2,1)S(1)}, bf16[32,1152]{1,0:T(8,128)(2,1)S(1)}, u32[]{:S(2)}, u32[]{:S(2)}) collective-permute-start(bf16[32,1152]{1,0:T(8,128)(2,1)S(1)} %get-tuple-element.29), channel_id=1, source_target_pairs={{0,64},{32,96},{64,0},{96,32},{1,65},{33,97},{65,1},{97,33},{2,66}... | collective-permute-start | bytes 221192 | tf_op jit(solution)/shard_map/ppermute | solution.py:32
  40.7 2.5 %collective-permute-done.9.by2 = bf16[32,1152]{1,0:T(8,128)(2,1)S(1)} collective-permute-done((bf16[32,1152]{1,0:T(8,128)(2,1)S(1)}, bf16[32,1152]{1,0:T(8,128)(2,1)S(1)}, u32[]{:S(2)}, u32[]{:S(2)}) %collective-permute-start.9) | collective-permute-done | bytes 73760 | tf_op jit(solution)/shard_map/ppermute | solution.py:32
  43.3 4.0 %collective-permute-start.11 = (bf16[32,1152]{1,0:T(8,128)(2,1)S(1)}, bf16[32,1152]{1,0:T(8,128)(2,1)S(1)}, u32[]{:S(2)}, u32[]{:S(2)}) collective-permute-start(bf16[32,1152]{1,0:T(8,128)(2,1)S(1)} %get-tuple-element.31), channel_id=1, source_target_pairs={{0,134},{2,132},{4,130},{6,128},{128,6},{130,4},{132,2},{134,0},{1... | collective-permute-start | bytes 221192 | tf_op jit(solution)/shard_map/ppermute | solution.py:304
  47.2 2.3 %collective-permute-done.11.theirs = bf16[32,1152]{1,0:T(8,128)(2,1)S(1)} collective-permute-done((bf16[32,1152]{1,0:T(8,128)(2,1)S(1)}, bf16[32,1152]{1,0:T(8,128)(2,1)S(1)}, u32[]{:S(2)}, u32[]{:S(2)}) %collective-permute-start.11) | collective-permute-done | bytes 73760 | tf_op jit(solution)/shard_map/ppermute | solution.py:304
  52.5 2.5 %collective-permute-start.14 = (bf16[1,32,576]{2,1,0:T(8,128)(2,1)S(1)}, bf16[1,32,576]{2,1,0:T(8,128)(2,1)S(1)}, u32[]{:S(2)}, u32[]{:S(2)}) collective-permute-start(bf16[1,32,576]{2,1,0:T(8,128)(2,1)S(1)} %shard_map.88), channel_id=1, source_target_pairs={{0,6},{2,4},{4,2},{6,0},{1,7},{3,5},{5,3},{7,1},{8,14},{10,12},{12... | collective-permute-start | bytes 110600 | tf_op jit(solution)/shard_map/ppermute | solution.py:32
  55.7 2.6 %collective-permute-done.14 = bf16[1,32,576]{2,1,0:T(8,128)(2,1)S(1)} collective-permute-done((bf16[1,32,576]{2,1,0:T(8,128)(2,1)S(1)}, bf16[1,32,576]{2,1,0:T(8,128)(2,1)S(1)}, u32[]{:S(2)}, u32[]{:S(2)}) %collective-permute-start.14) | collective-permute-done | bytes 36896 | tf_op jit(solution)/shard_map/ppermute | solution.py:32
  58.5 3.5 %collective-permute-start.16 = (bf16[4,32,576]{2,1,0:T(8,128)(2,1)S(1)}, bf16[4,32,576]{2,1,0:T(8,128)(2,1)S(1)}, u32[]{:S(2)}, u32[]{:S(2)}) collective-permute-start(bf16[4,32,576]{2,1,0:T(8,128)(2,1)S(1)} %pad_maximum_fusion), channel_id=1, source_target_pairs={{0,16},{8,24},{16,0},{24,8},{1,17},{9,25},{17,1},{25,9},{2,18},{10... | collective-permute-start | bytes 442376 | tf_op jit(solution)/shard_map/ppermute | solution.py:32
  63.8 3.2 %collective-permute-done.16 = bf16[4,32,576]{2,1,0:T(8,128)(2,1)S(1)} collective-permute-done((bf16[4,32,576]{2,1,0:T(8,128)(2,1)S(1)}, bf16[4,32,576]{2,1,0:T(8,128)(2,1)S(1)}, u32[]{:S(2)}, u32[]{:S(2)}) %collective-permute-start.16) | collective-permute-done | bytes 147488 | tf_op jit(solution)/shard_map/ppermute | solution.py:32
  88.4 5.6 %collective-permute-start.22 = (bf16[2,128,256]{2,1,0:T(8,128)(2,1)S(1)}, bf16[2,128,256]{2,1,0:T(8,128)(2,1)S(1)}, u32[]{:S(2)}, u32[]{:S(2)}) collective-permute-start(bf16[2,128,256]{2,1,0:T(8,128)(2,1)S(1)} %get-tuple-element.41.after), channel_id=1, source_target_pairs={{0,128},{128,0},{1,129},{129,1},{2,130},{130,2},{3,131},{131,3},{4... | collective-permute-start | bytes 393224 | tf_op jit(solution)/shard_map/ppermute | solution.py:32
  95.7 5.2 %collective-permute-start.30 = (bf16[2,128,256]{2,1,0:T(8,128)(2,1)S(1)}, bf16[2,128,256]{2,1,0:T(8,128)(2,1)S(1)}, u32[]{:S(2)}, u32[]{:S(2)}) collective-permute-start(bf16[2,128,256]{2,1,0:T(8,128)(2,1)S(1)} %get-tuple-element.51), channel_id=1, source_target_pairs={{0,128},{128,0},{1,129},{129,1},{2,130},{130,2},{3,131},{131,3},{4... | collective-permute-start | bytes 393224 | tf_op jit(solution)/shard_map/ppermute | solution.py:32
  101.7 5.3 %collective-permute-done.26.theirs = bf16[2,128,256]{2,1,0:T(8,128)(2,1)S(1)} collective-permute-done((bf16[2,128,256]{2,1,0:T(8,128)(2,1)S(1)}, bf16[2,128,256]{2,1,0:T(8,128)(2,1)S(1)}, u32[]{:S(2)}, u32[]{:S(2)}) %collective-permute-start.26) | collective-permute-done | bytes 131104 | tf_op jit(solution)/shard_map/ppermute | solution.py:32
  107.7 3.2 %collective-permute-start.34 = (bf16[2,128,256]{2,1,0:T(8,128)(2,1)S(1)}, bf16[2,128,256]{2,1,0:T(8,128)(2,1)S(1)}, u32[]{:S(2)}, u32[]{:S(2)}) collective-permute-start(bf16[2,128,256]{2,1,0:T(8,128)(2,1)S(1)} %shard_map.96.after.lat1.refs_4_), channel_id=1, source_target_pairs={{0,32},{32,0},{64,96},{96,64},{1,33},{33,1},{65,97},{97,65},{2,34}... | collective-permute-start | bytes 393224 | tf_op jit(solution)/shard_map/ppermute | solution.py:32
  110.9 2.3 %collective-permute-start.35 = (bf16[2,128,256]{2,1,0:T(8,128)(2,1)S(1)}, bf16[2,128,256]{2,1,0:T(8,128)(2,1)S(1)}, u32[]{:S(2)}, u32[]{:S(2)}) collective-permute-start(bf16[2,128,256]{2,1,0:T(8,128)(2,1)S(1)} %shard_map.96.after.lat1.refs_4_), channel_id=1, source_target_pairs={{0,64},{32,96},{64,0},{96,32},{1,65},{33,97},{65,1},{97,33},{2,66}... | collective-permute-start | bytes 393224 | tf_op jit(solution)/shard_map/ppermute | solution.py:32
  113.1 2.4 %collective-permute-start.31 = (bf16[2,128,256]{2,1,0:T(8,128)(2,1)S(1)}, bf16[2,128,256]{2,1,0:T(8,128)(2,1)S(1)}, u32[]{:S(2)}, u32[]{:S(2)}) collective-permute-start(bf16[2,128,256]{2,1,0:T(8,128)(2,1)S(1)} %shard_map.94.after.lat0.refs_0_), channel_id=1, source_target_pairs={{0,32},{32,0},{64,96},{96,64},{1,33},{33,1},{65,97},{97,65},{2,34}... | collective-permute-start | bytes 393224 | tf_op jit(solution)/shard_map/ppermute | solution.py:32
  121.7 2.7 %collective-permute-start.38 = (bf16[2,128,256]{2,1,0:T(8,128)(2,1)S(1)}, bf16[2,128,256]{2,1,0:T(8,128)(2,1)S(1)}, u32[]{:S(2)}, u32[]{:S(2)}) collective-permute-start(bf16[2,128,256]{2,1,0:T(8,128)(2,1)S(1)} %shard_map.98.lat2.after.l0), channel_id=1, source_target_pairs={{0,64},{32,96},{64,0},{96,32},{1,65},{33,97},{65,1},{97,33},{2,66}... | collective-permute-start | bytes 393224 | tf_op jit(solution)/shard_map/ppermute | solution.py:32
  126.7 2.2 %shard_map.100.total = f32[4,2,128,576]{3,2,1,0:T(8,128)S(1)} custom-call(s32[5]{0:T(128)S(1)} %stack.23.pos, s32[8,16]{1,0:T(8,128)S(1)} %pad_add_fusion.tab, bf16[2,128,256]{2,1,0:T(8,128)(2,1)S(1)} %shard_map.98.lat2.after.l0, bf16[2,128,256]{2,1,0:T(8,128)(2,1)S(1)} %shard_map.94.after.lat0.refs_0_, ...), custom_call_target="tpu_custom_call" | custom-call | flops 603979776 | bytes 5000000 | tf_op jit(solution)/shard_map/pallas_call | solution.py:41
  131.3 2.1 %collective-permute-done.40.theirs = bf16[4,4,32,576]{3,2,1,0:T(8,128)(2,1)S(1)} collective-permute-done((bf16[4,4,32,576]{3,2,1,0:T(8,128)(2,1)S(1)}, bf16[4,4,32,576]{3,2,1,0:T(8,128)(2,1)S(1)}, u32[]{:S(2)}, u32[]{:S(2)}) %collective-permute-start.40) | collective-permute-done | bytes 589856 | tf_op jit(solution)/shard_map/ppermute | solution.py:32
  134.3 3.6 %all-to-all-start = ((bf16[16,32,576]{2,1,0:T(8,128)(2,1)}), bf16[16,32,576]{2,1,0:T(8,128)(2,1)S(1)}, u32[]{:S(2)}, u32[]{:S(2)}) async-start(bf16[16,32,576]{2,1,0:T(8,128)(2,1)} %bitcast.10), calls=%async_computation | async-start | bytes 1310720 | tf_op jit(solution)/shard_map/all_to_all | solution.py:396
  139.5 18.3 %all-to-all-done.parts = bf16[16,32,576]{2,1,0:T(8,128)(2,1)S(1)} async-done(((bf16[16,32,576]{2,1,0:T(8,128)(2,1)}), bf16[16,32,576]{2,1,0:T(8,128)(2,1)S(1)}, u32[]{:S(2)}, u32[]{:S(2)}) %all-to-all-start) | async-done | bytes 589856 | tf_op jit(solution)/shard_map/all_to_all | solution.py:396
  (117 shorter events, 58.2 us)
Async XLA Ops:
  0.6 10.1 %collective-permute-start = (bf16[144,128]{1,0:T(8,128)(2,1)}, bf16[144,128]{1,0:T(8,128)(2,1)S(1)}, u32[]{:S(2)}, u32[]{:S(2)}) collective-permute-start(bf16[144,128]{1,0:T(8,128)(2,1)} %bitcast.22), channel_id=1, source_target_pairs={{0,16},{1,17},{2,18},{3,19},{4,60},{5,61},{6,62},{7,63},{8,72},{9,... | collective-permute-start | bytes 110600 | tf_op jit(solution)/shard_map/ppermute | solution.py:278
  18.7 9.4 %collective-permute-start.5 = (bf16[4,144,128]{2,1,0:T(8,128)(2,1)S(1)}, bf16[4,144,128]{2,1,0:T(8,128)(2,1)S(1)}, u32[]{:S(2)}, u32[]{:S(2)}) collective-permute-start(bf16[4,144,128]{2,1,0:T(8,128)(2,1)S(1)} %pad_maximum_fusion.1), channel_id=1, source_target_pairs={{0,16},{8,24},{16,0},{24,8},{1,17},{9,25},{17,1},{25,9},{2,18},{10... | collective-permute-start | bytes 442376 | tf_op jit(solution)/shard_map/ppermute | solution.py:32
  58.5 8.6 %collective-permute-start.16 = (bf16[4,32,576]{2,1,0:T(8,128)(2,1)S(1)}, bf16[4,32,576]{2,1,0:T(8,128)(2,1)S(1)}, u32[]{:S(2)}, u32[]{:S(2)}) collective-permute-start(bf16[4,32,576]{2,1,0:T(8,128)(2,1)S(1)} %pad_maximum_fusion), channel_id=1, source_target_pairs={{0,16},{8,24},{16,0},{24,8},{1,17},{9,25},{17,1},{25,9},{2,18},{10... | collective-permute-start | bytes 442376 | tf_op jit(solution)/shard_map/ppermute | solution.py:32
  72.7 8.3 %collective-permute-start.19 = (bf16[2,128,256]{2,1,0:T(8,128)(2,1)S(1)}, bf16[2,128,256]{2,1,0:T(8,128)(2,1)S(1)}, u32[]{:S(2)}, u32[]{:S(2)}) collective-permute-start(bf16[2,128,256]{2,1,0:T(8,128)(2,1)S(1)} %get-tuple-element.37), channel_id=1, source_target_pairs={{0,64},{32,96},{64,0},{96,32},{1,65},{33,97},{65,1},{97,33},{2,66}... | collective-permute-start | bytes 393224 | tf_op jit(solution)/shard_map/ppermute | solution.py:32
  74.1 10.0 %collective-permute-start.20 = (bf16[2,128,256]{2,1,0:T(8,128)(2,1)S(1)}, bf16[2,128,256]{2,1,0:T(8,128)(2,1)S(1)}, u32[]{:S(2)}, u32[]{:S(2)}) collective-permute-start(bf16[2,128,256]{2,1,0:T(8,128)(2,1)S(1)} %get-tuple-element.38), channel_id=1, source_target_pairs={{0,32},{32,0},{64,96},{96,64},{1,33},{33,1},{65,97},{97,65},{2,34}... | collective-permute-start | bytes 393224 | tf_op jit(solution)/shard_map/ppermute | solution.py:32
  75.3 10.3 %collective-permute-start.21 = (bf16[2,128,256]{2,1,0:T(8,128)(2,1)S(1)}, bf16[2,128,256]{2,1,0:T(8,128)(2,1)S(1)}, u32[]{:S(2)}, u32[]{:S(2)}) collective-permute-start(bf16[2,128,256]{2,1,0:T(8,128)(2,1)S(1)} %get-tuple-element.39), channel_id=1, source_target_pairs={{0,96},{32,64},{64,32},{96,0},{1,97},{33,65},{65,33},{97,1},{2,98}... | collective-permute-start | bytes 393224 | tf_op jit(solution)/shard_map/ppermute | solution.py:32
  78.4 8.3 %collective-permute-start.23 = (bf16[2,128,256]{2,1,0:T(8,128)(2,1)S(1)}, bf16[2,128,256]{2,1,0:T(8,128)(2,1)S(1)}, u32[]{:S(2)}, u32[]{:S(2)}) collective-permute-start(bf16[2,128,256]{2,1,0:T(8,128)(2,1)S(1)} %get-tuple-element.42), channel_id=1, source_target_pairs={{0,64},{32,96},{64,0},{96,32},{1,65},{33,97},{65,1},{97,33},{2,66}... | collective-permute-start | bytes 393224 | tf_op jit(solution)/shard_map/ppermute | solution.py:32
  79.8 8.6 %collective-permute-start.24 = (bf16[2,128,256]{2,1,0:T(8,128)(2,1)S(1)}, bf16[2,128,256]{2,1,0:T(8,128)(2,1)S(1)}, u32[]{:S(2)}, u32[]{:S(2)}) collective-permute-start(bf16[2,128,256]{2,1,0:T(8,128)(2,1)S(1)} %get-tuple-element.43), channel_id=1, source_target_pairs={{0,32},{32,0},{64,96},{96,64},{1,33},{33,1},{65,97},{97,65},{2,34}... | collective-permute-start | bytes 393224 | tf_op jit(solution)/shard_map/ppermute | solution.py:32
  81.0 13.1 %collective-permute-start.25 = (bf16[2,128,256]{2,1,0:T(8,128)(2,1)S(1)}, bf16[2,128,256]{2,1,0:T(8,128)(2,1)S(1)}, u32[]{:S(2)}, u32[]{:S(2)}) collective-permute-start(bf16[2,128,256]{2,1,0:T(8,128)(2,1)S(1)} %get-tuple-element.44), channel_id=1, source_target_pairs={{0,96},{32,64},{64,32},{96,0},{1,97},{33,65},{65,33},{97,1},{2,98}... | collective-permute-start | bytes 393224 | tf_op jit(solution)/shard_map/ppermute | solution.py:32
  84.1 11.5 %collective-permute-start.27 = (bf16[2,128,256]{2,1,0:T(8,128)(2,1)S(1)}, bf16[2,128,256]{2,1,0:T(8,128)(2,1)S(1)}, u32[]{:S(2)}, u32[]{:S(2)}) collective-permute-start(bf16[2,128,256]{2,1,0:T(8,128)(2,1)S(1)} %get-tuple-element.47), channel_id=1, source_target_pairs={{0,64},{32,96},{64,0},{96,32},{1,65},{33,97},{65,1},{97,33},{2,66}... | collective-permute-start | bytes 393224 | tf_op jit(solution)/shard_map/ppermute | solution.py:32
  85.6 10.1 %collective-permute-start.28 = (bf16[2,128,256]{2,1,0:T(8,128)(2,1)S(1)}, bf16[2,128,256]{2,1,0:T(8,128)(2,1)S(1)}, u32[]{:S(2)}, u32[]{:S(2)}) collective-permute-start(bf16[2,128,256]{2,1,0:T(8,128)(2,1)S(1)} %get-tuple-element.48), channel_id=1, source_target_pairs={{0,32},{32,0},{64,96},{96,64},{1,33},{33,1},{65,97},{97,65},{2,34}... | collective-permute-start | bytes 393224 | tf_op jit(solution)/shard_map/ppermute | solution.py:32
  86.7 9.0 %collective-permute-start.29 = (bf16[2,128,256]{2,1,0:T(8,128)(2,1)S(1)}, bf16[2,128,256]{2,1,0:T(8,128)(2,1)S(1)}, u32[]{:S(2)}, u32[]{:S(2)}) collective-permute-start(bf16[2,128,256]{2,1,0:T(8,128)(2,1)S(1)} %get-tuple-element.49), channel_id=1, source_target_pairs={{0,96},{32,64},{64,32},{96,0},{1,97},{33,65},{65,33},{97,1},{2,98}... | collective-permute-start | bytes 393224 | tf_op jit(solution)/shard_map/ppermute | solution.py:32
  88.4 12.7 %collective-permute-start.22 = (bf16[2,128,256]{2,1,0:T(8,128)(2,1)S(1)}, bf16[2,128,256]{2,1,0:T(8,128)(2,1)S(1)}, u32[]{:S(2)}, u32[]{:S(2)}) collective-permute-start(bf16[2,128,256]{2,1,0:T(8,128)(2,1)S(1)} %get-tuple-element.41.after), channel_id=1, source_target_pairs={{0,128},{128,0},{1,129},{129,1},{2,130},{130,2},{3,131},{131,3},{4... | collective-permute-start | bytes 393224 | tf_op jit(solution)/shard_map/ppermute | solution.py:32
  94.1 12.9 %collective-permute-start.26 = (bf16[2,128,256]{2,1,0:T(8,128)(2,1)S(1)}, bf16[2,128,256]{2,1,0:T(8,128)(2,1)S(1)}, u32[]{:S(2)}, u32[]{:S(2)}) collective-permute-start(bf16[2,128,256]{2,1,0:T(8,128)(2,1)S(1)} %get-tuple-element.46.after), channel_id=1, source_target_pairs={{0,128},{128,0},{1,129},{129,1},{2,130},{130,2},{3,131},{131,3},{4... | collective-permute-start | bytes 393224 | tf_op jit(solution)/shard_map/ppermute | solution.py:32
  95.7 19.8 %collective-permute-start.30 = (bf16[2,128,256]{2,1,0:T(8,128)(2,1)S(1)}, bf16[2,128,256]{2,1,0:T(8,128)(2,1)S(1)}, u32[]{:S(2)}, u32[]{:S(2)}) collective-permute-start(bf16[2,128,256]{2,1,0:T(8,128)(2,1)S(1)} %get-tuple-element.51), channel_id=1, source_target_pairs={{0,128},{128,0},{1,129},{129,1},{2,130},{130,2},{3,131},{131,3},{4... | collective-permute-start | bytes 393224 | tf_op jit(solution)/shard_map/ppermute | solution.py:32
  107.7 8.9 %collective-permute-start.34 = (bf16[2,128,256]{2,1,0:T(8,128)(2,1)S(1)}, bf16[2,128,256]{2,1,0:T(8,128)(2,1)S(1)}, u32[]{:S(2)}, u32[]{:S(2)}) collective-permute-start(bf16[2,128,256]{2,1,0:T(8,128)(2,1)S(1)} %shard_map.96.after.lat1.refs_4_), channel_id=1, source_target_pairs={{0,32},{32,0},{64,96},{96,64},{1,33},{33,1},{65,97},{97,65},{2,34}... | collective-permute-start | bytes 393224 | tf_op jit(solution)/shard_map/ppermute | solution.py:32
  110.9 9.2 %collective-permute-start.35 = (bf16[2,128,256]{2,1,0:T(8,128)(2,1)S(1)}, bf16[2,128,256]{2,1,0:T(8,128)(2,1)S(1)}, u32[]{:S(2)}, u32[]{:S(2)}) collective-permute-start(bf16[2,128,256]{2,1,0:T(8,128)(2,1)S(1)} %shard_map.96.after.lat1.refs_4_), channel_id=1, source_target_pairs={{0,64},{32,96},{64,0},{96,32},{1,65},{33,97},{65,1},{97,33},{2,66}... | collective-permute-start | bytes 393224 | tf_op jit(solution)/shard_map/ppermute | solution.py:32
  113.1 8.6 %collective-permute-start.36 = (bf16[2,128,256]{2,1,0:T(8,128)(2,1)S(1)}, bf16[2,128,256]{2,1,0:T(8,128)(2,1)S(1)}, u32[]{:S(2)}, u32[]{:S(2)}) collective-permute-start(bf16[2,128,256]{2,1,0:T(8,128)(2,1)S(1)} %shard_map.96.after.lat1.refs_4_), channel_id=1, source_target_pairs={{0,96},{32,64},{64,32},{96,0},{1,97},{33,65},{65,33},{97,1},{2,98}... | collective-permute-start | bytes 393224 | tf_op jit(solution)/shard_map/ppermute | solution.py:32
  113.1 11.3 %collective-permute-start.31 = (bf16[2,128,256]{2,1,0:T(8,128)(2,1)S(1)}, bf16[2,128,256]{2,1,0:T(8,128)(2,1)S(1)}, u32[]{:S(2)}, u32[]{:S(2)}) collective-permute-start(bf16[2,128,256]{2,1,0:T(8,128)(2,1)S(1)} %shard_map.94.after.lat0.refs_0_), channel_id=1, source_target_pairs={{0,32},{32,0},{64,96},{96,64},{1,33},{33,1},{65,97},{97,65},{2,34}... | collective-permute-start | bytes 393224 | tf_op jit(solution)/shard_map/ppermute | solution.py:32
  115.6 9.8 %collective-permute-start.32 = (bf16[2,128,256]{2,1,0:T(8,128)(2,1)S(1)}, bf16[2,128,256]{2,1,0:T(8,128)(2,1)S(1)}, u32[]{:S(2)}, u32[]{:S(2)}) collective-permute-start(bf16[2,128,256]{2,1,0:T(8,128)(2,1)S(1)} %shard_map.94.after.lat0.refs_0_), channel_id=1, source_target_pairs={{0,64},{32,96},{64,0},{96,32},{1,65},{33,97},{65,1},{97,33},{2,66}... | collective-permute-start | bytes 393224 | tf_op jit(solution)/shard_map/ppermute | solution.py:32
  116.6 10.0 %collective-permute-start.33 = (bf16[2,128,256]{2,1,0:T(8,128)(2,1)S(1)}, bf16[2,128,256]{2,1,0:T(8,128)(2,1)S(1)}, u32[]{:S(2)}, u32[]{:S(2)}) collective-permute-start(bf16[2,128,256]{2,1,0:T(8,128)(2,1)S(1)} %shard_map.94.after.lat0.refs_0_), channel_id=1, source_target_pairs={{0,96},{32,64},{64,32},{96,0},{1,97},{33,65},{65,33},{97,1},{2,98}... | collective-permute-start | bytes 393224 | tf_op jit(solution)/shard_map/ppermute | solution.py:32
  120.0 8.8 %collective-permute-start.37 = (bf16[2,128,256]{2,1,0:T(8,128)(2,1)S(1)}, bf16[2,128,256]{2,1,0:T(8,128)(2,1)S(1)}, u32[]{:S(2)}, u32[]{:S(2)}) collective-permute-start(bf16[2,128,256]{2,1,0:T(8,128)(2,1)S(1)} %shard_map.98.lat2.after.l0), channel_id=1, source_target_pairs={{0,32},{32,0},{64,96},{96,64},{1,33},{33,1},{65,97},{97,65},{2,34}... | collective-permute-start | bytes 393224 | tf_op jit(solution)/shard_map/ppermute | solution.py:32
  121.7 7.2 %collective-permute-start.38 = (bf16[2,128,256]{2,1,0:T(8,128)(2,1)S(1)}, bf16[2,128,256]{2,1,0:T(8,128)(2,1)S(1)}, u32[]{:S(2)}, u32[]{:S(2)}) collective-permute-start(bf16[2,128,256]{2,1,0:T(8,128)(2,1)S(1)} %shard_map.98.lat2.after.l0), channel_id=1, source_target_pairs={{0,64},{32,96},{64,0},{96,32},{1,65},{33,97},{65,1},{97,33},{2,66}... | collective-permute-start | bytes 393224 | tf_op jit(solution)/shard_map/ppermute | solution.py:32
  134.3 23.5 %all-to-all-start = ((bf16[16,32,576]{2,1,0:T(8,128)(2,1)}), bf16[16,32,576]{2,1,0:T(8,128)(2,1)S(1)}, u32[]{:S(2)}, u32[]{:S(2)}) async-start(bf16[16,32,576]{2,1,0:T(8,128)(2,1)} %bitcast.10), calls=%async_computation | async-start | bytes 1310720 | tf_op jit(solution)/shard_map/all_to_all | solution.py:396
  (23 other events, 231.8 us)
where the time goes:
time: 161 us; the launch traced here: 159 us
  starting transfers between devices  74.1 us (46%)
  waiting for transfers between devices  63.9 us (40%)
  Pallas kernels  16.8 us (10%)
  other arithmetic  2.51 us (2%)
    ppermute x39, starting transfers between devices, swap(): return lax.ppermute(value, axis, [(i, i ^ k) for i in range(SIZES[axis])])  64.9 us
    ppermute x39, waiting for transfers between devices, swap(): return lax.ppermute(value, axis, [(i, i ^ k) for i in range(SIZES[axis])])  34.8 us
    all_to_all x1, waiting for transfers between devices, shards(): lax.all_to_all(joined, ('y', 'zl'), 0, 0, tiled=True)  18.3 us
    pallas_call x18, Pallas kernels, call(): pl.pallas_call(kernel, out_shape=outs, in_specs=specs, out_specs=jax.tree...  16.8 us
    ppermute x1, waiting for transfers between devices, shards(): own = lax.ppermute(residual.T, ROWS + LAT, pairs)  8.46 us
    ppermute x1, starting transfers between devices, shards(): theirs = lax.ppermute(narrow, ('zh', 'zl'), [(i, 7 - i) for i in range(8)])  3.98 us
    all_to_all x1, starting transfers between devices, shards(): lax.all_to_all(joined, ('y', 'zl'), 0, 0, tiled=True)  3.59 us
  transfers between devices with their start and end apart: 42, of which 25 were waited for; matrix products, arithmetic and copies ran while one was open for 2% of the time, Pallas kernels for 6%

commit v1 on v0

--- a/solution.py
+++ b/solution.py
@@ -224,27 +224,27 @@
 
 
 def finish_kernel(pos, tab, total, l0, l1, l2, l3, weight, mine, theirs):
-    _, x, _, _, _ = bits(pos)
+    _, x, y, zl, _ = bits(pos)
     for k, lat in enumerate((l0, l1, l2, l3)):
         xb = x ^ k
         for zb in range(2):
             acc = total[k, zb] + decode_pair(2, tab, lat, zb, zb * 4 + xb, weight)
-            ky = zb * 2 + xb // 2
+            ky = (zb * 2 + xb // 2) ^ y
             for q in range(2):
-                kz = (xb & 1) * 2 + q
+                kz = ((xb & 1) * 2 + q) ^ zl
                 mine[ky, kz] = acc[q * SUB : (q + 1) * SUB]
                 theirs[ky, kz] = acc[64 + q * SUB : 64 + (q + 1) * SUB].astype(BF16)
 
 
-def join_kernel(mine, theirs, out):
-    out[...] = (mine[...] + theirs[...].astype(F32)).astype(BF16)
-
-
-def total_kernel(parts, bias, out):
-    total = parts[0].astype(F32)
-    for i in range(1, 16):
-        total = total + parts[i].astype(F32)
-    out[...] = (total + bias[...]).astype(BF16)
+def join_kernel(mine, theirs, wide, s1, s2, s3):
+    for k, out in enumerate((wide, s1, s2, s3)):
+        out[...] = (mine[k] + theirs[k].astype(F32)).astype(out.dtype)
+
+
+def fold_kernel(p0, p1, p2, p3, wide, s1, s2, s3):
+    for k, out in enumerate((wide, s1, s2, s3)):
+        total = p0[k] + p1[k].astype(F32) + p2[k].astype(F32) + p3[k].astype(F32)
+        out[...] = total.astype(out.dtype)
 
 
 def tables(active_blocks, lat_index):
@@ -387,16 +387,26 @@
         [SMEM, SMEM] + [VMEM] * 3,
         size=1000000,
     )
-    joined = call(
-        join_kernel, jax.ShapeDtypeStruct(part, BF16), (mine, swap(theirs, "c", 1)), [VMEM] * 2, size=4000000
-    ).reshape(16, SUB, SLICE)
-    recon = call(
-        total_kernel,
-        jax.ShapeDtypeStruct((SUB, SLICE), BF16),
-        (lax.all_to_all(joined, ("y", "zl"), 0, 0, tiled=True), dec_bias.reshape(1, SLICE)),
+    quarter = jax.ShapeDtypeStruct(part[1:], BF16)
+    p0, p1, p2, p3 = call(
+        join_kernel,
+        (jax.ShapeDtypeStruct(part[1:], F32), quarter, quarter, quarter),
+        (mine, swap(theirs, "c", 1)),
         [VMEM] * 2,
-        size=600000,
-    )
+        size=3000000,
+    )
+    q2, q1, q3 = swap(p2, "y", 2), swap(p1, "y", 1), swap(p3, "y", 3)
+    small = jax.ShapeDtypeStruct((SUB, SLICE), BF16)
+    recon, s1, s2, s3 = call(
+        fold_kernel,
+        (jax.ShapeDtypeStruct((SUB, SLICE), F32), small, small, small),
+        (p0, q1, q2, q3),
+        [VMEM] * 4,
+        size=1000000,
+    )
+    r2, r1, r3 = swap(s2, "zl", 2), swap(s1, "zl", 1), swap(s3, "zl", 3)
+    recon = recon + r1.astype(F32) + r2.astype(F32) + r3.astype(F32)
+    recon = (recon + dec_bias).astype(BF16)
     return latents, recon
 
 

time: 161 us -> 157 us (0.975)
  waiting for transfers between devices: 63.9 us -> 55.9 us
  starting transfers between devices: 74.1 us -> 79.7 us
    all_to_all x1 -> x0, waiting for transfers between devices: 18.3 us -> none  [shards(): lax.all_to_all(joined, ('y', 'zl'), 0, 0, tiled=True)]
    ppermute x39 -> x45, waiting for transfers between devices: 34.8 us -> 45.1 us  [swap(): return lax.ppermute(value, axis, [(i, i ^ k) for i in range(SIZES[axis])])]
    ppermute x39 -> x45, starting transfers between devices: 64.9 us -> 74.1 us  [swap(): return lax.ppermute(value, axis, [(i, i ^ k) for i in range(SIZES[axis])])]
    all_to_all x1 -> x0, starting transfers between devices: 3.59 us -> none  [shards(): lax.all_to_all(joined, ('y', 'zl'), 0, 0, tiled=True)]
  transfers between devices with their start and end apart: 42 -> 47, of which waited for: 25 -> 28; matrix products, arithmetic and copies ran while one was open for 2% -> 2% of each run, Pallas kernels for 6% -> 6%
where the time goes in v1:
time: 157 us; the launch traced here: 155 us
  starting transfers between devices  79.7 us (51%)
  waiting for transfers between devices  55.9 us (36%)
  Pallas kernels  15.3 us (10%)
  other arithmetic  3.15 us (2%)
    ppermute x45, starting transfers between devices, swap(): return lax.ppermute(value, axis, [(i, i ^ k) for i in range(SIZES[axis])])  74.1 us
    ppermute x45, waiting for transfers between devices, swap(): return lax.ppermute(value, axis, [(i, i ^ k) for i in range(SIZES[axis])])  45.1 us
    pallas_call x18, Pallas kernels, call(): pl.pallas_call(kernel, out_shape=outs, in_specs=specs, out_specs=jax.tree...  15.3 us
    ppermute x1, waiting for transfers between devices, shards(): own = lax.ppermute(residual.T, ROWS + LAT, pairs)  8.46 us
    ppermute x1, starting transfers between devices, shards(): theirs = lax.ppermute(narrow, ('zh', 'zl'), [(i, 7 - i) for i in range(8)])  3.98 us
  transfers between devices with their start and end apart: 47, of which 28 were waited for; matrix products, arithmetic and copies ran while one was open for 2% of the time, Pallas kernels for 6%

profile of v1, /device:TPU:2, one launch (start us, length us, event | category | flops | bytes accessed | tf_op | source)
XLA Modules:
  0.0 155.4 jit_solution(8112572804341494218)
XLA Ops:
  2.3 8.5 %collective-permute-done = bf16[144,128]{1,0:T(8,128)(2,1)S(1)} collective-permute-done((bf16[144,128]{1,0:T(8,128)(2,1)}, bf16[144,128]{1,0:T(8,128)(2,1)S(1)}, u32[]{:S(2)}, u32[]{:S(2)}) %collective-permute-start) | collective-permute-done | bytes 36896 | tf_op jit(solution)/shard_map/ppermute | solution.py:278
  11.7 3.4 %collective-permute-start.3 = (bf16[1,144,128]{2,1,0:T(8,128)(2,1)S(1)}, bf16[1,144,128]{2,1,0:T(8,128)(2,1)S(1)}, u32[]{:S(2)}, u32[]{:S(2)}) collective-permute-start(bf16[1,144,128]{2,1,0:T(8,128)(2,1)S(1)} %bitcast.19), channel_id=1, source_target_pairs={{0,6},{2,4},{4,2},{6,0},{1,7},{3,5},{5,3},{7,1},{8,14},{10,12},{12... | collective-permute-start | bytes 110600 | tf_op jit(solution)/shard_map/ppermute | solution.py:32
  18.7 4.7 %collective-permute-start.5 = (bf16[4,144,128]{2,1,0:T(8,128)(2,1)S(1)}, bf16[4,144,128]{2,1,0:T(8,128)(2,1)S(1)}, u32[]{:S(2)}, u32[]{:S(2)}) collective-permute-start(bf16[4,144,128]{2,1,0:T(8,128)(2,1)S(1)} %pad_maximum_fusion.1), channel_id=1, source_target_pairs={{0,16},{8,24},{16,0},{24,8},{1,17},{9,25},{17,1},{25,9},{2,18},{10... | collective-permute-start | bytes 442376 | tf_op jit(solution)/shard_map/ppermute | solution.py:32
  24.1 4.0 %collective-permute-done.5 = bf16[4,144,128]{2,1,0:T(8,128)(2,1)S(1)} collective-permute-done((bf16[4,144,128]{2,1,0:T(8,128)(2,1)S(1)}, bf16[4,144,128]{2,1,0:T(8,128)(2,1)S(1)}, u32[]{:S(2)}, u32[]{:S(2)}) %collective-permute-start.5) | collective-permute-done | bytes 147488 | tf_op jit(solution)/shard_map/ppermute | solution.py:32
  33.1 3.2 %collective-permute-start.10 = (bf16[32,1152]{1,0:T(8,128)(2,1)S(1)}, bf16[32,1152]{1,0:T(8,128)(2,1)S(1)}, u32[]{:S(2)}, u32[]{:S(2)}) collective-permute-start(bf16[32,1152]{1,0:T(8,128)(2,1)S(1)} %get-tuple-element.37), channel_id=1, source_target_pairs={{0,96},{32,64},{64,32},{96,0},{1,97},{33,65},{65,33},{97,1},{2,98}... | collective-permute-start | bytes 221192 | tf_op jit(solution)/shard_map/ppermute | solution.py:32
  40.7 2.5 %collective-permute-done.9.by2 = bf16[32,1152]{1,0:T(8,128)(2,1)S(1)} collective-permute-done((bf16[32,1152]{1,0:T(8,128)(2,1)S(1)}, bf16[32,1152]{1,0:T(8,128)(2,1)S(1)}, u32[]{:S(2)}, u32[]{:S(2)}) %collective-permute-start.9) | collective-permute-done | bytes 73760 | tf_op jit(solution)/shard_map/ppermute | solution.py:32
  43.3 4.0 %collective-permute-start.11 = (bf16[32,1152]{1,0:T(8,128)(2,1)S(1)}, bf16[32,1152]{1,0:T(8,128)(2,1)S(1)}, u32[]{:S(2)}, u32[]{:S(2)}) collective-permute-start(bf16[32,1152]{1,0:T(8,128)(2,1)S(1)} %get-tuple-element.39), channel_id=1, source_target_pairs={{0,134},{2,132},{4,130},{6,128},{128,6},{130,4},{132,2},{134,0},{1... | collective-permute-start | bytes 221192 | tf_op jit(solution)/shard_map/ppermute | solution.py:304
  47.2 2.3 %collective-permute-done.11.theirs = bf16[32,1152]{1,0:T(8,128)(2,1)S(1)} collective-permute-done((bf16[32,1152]{1,0:T(8,128)(2,1)S(1)}, bf16[32,1152]{1,0:T(8,128)(2,1)S(1)}, u32[]{:S(2)}, u32[]{:S(2)}) %collective-permute-start.11) | collective-permute-done | bytes 73760 | tf_op jit(solution)/shard_map/ppermute | solution.py:304
  52.5 2.5 %collective-permute-start.14 = (bf16[1,32,576]{2,1,0:T(8,128)(2,1)S(1)}, bf16[1,32,576]{2,1,0:T(8,128)(2,1)S(1)}, u32[]{:S(2)}, u32[]{:S(2)}) collective-permute-start(bf16[1,32,576]{2,1,0:T(8,128)(2,1)S(1)} %shard_map.88), channel_id=1, source_target_pairs={{0,6},{2,4},{4,2},{6,0},{1,7},{3,5},{5,3},{7,1},{8,14},{10,12},{12... | collective-permute-start | bytes 110600 | tf_op jit(solution)/shard_map/ppermute | solution.py:32
  55.7 2.6 %collective-permute-done.14 = bf16[1,32,576]{2,1,0:T(8,128)(2,1)S(1)} collective-permute-done((bf16[1,32,576]{2,1,0:T(8,128)(2,1)S(1)}, bf16[1,32,576]{2,1,0:T(8,128)(2,1)S(1)}, u32[]{:S(2)}, u32[]{:S(2)}) %collective-permute-start.14) | collective-permute-done | bytes 36896 | tf_op jit(solution)/shard_map/ppermute | solution.py:32
  58.5 3.5 %collective-permute-start.16 = (bf16[4,32,576]{2,1,0:T(8,128)(2,1)S(1)}, bf16[4,32,576]{2,1,0:T(8,128)(2,1)S(1)}, u32[]{:S(2)}, u32[]{:S(2)}) collective-permute-start(bf16[4,32,576]{2,1,0:T(8,128)(2,1)S(1)} %pad_maximum_fusion), channel_id=1, source_target_pairs={{0,16},{8,24},{16,0},{24,8},{1,17},{9,25},{17,1},{25,9},{2,18},{10... | collective-permute-start | bytes 442376 | tf_op jit(solution)/shard_map/ppermute | solution.py:32
  63.8 3.2 %collective-permute-done.16 = bf16[4,32,576]{2,1,0:T(8,128)(2,1)S(1)} collective-permute-done((bf16[4,32,576]{2,1,0:T(8,128)(2,1)S(1)}, bf16[4,32,576]{2,1,0:T(8,128)(2,1)S(1)}, u32[]{:S(2)}, u32[]{:S(2)}) %collective-permute-start.16) | collective-permute-done | bytes 147488 | tf_op jit(solution)/shard_map/ppermute | solution.py:32
  88.4 5.6 %collective-permute-start.22 = (bf16[2,128,256]{2,1,0:T(8,128)(2,1)S(1)}, bf16[2,128,256]{2,1,0:T(8,128)(2,1)S(1)}, u32[]{:S(2)}, u32[]{:S(2)}) collective-permute-start(bf16[2,128,256]{2,1,0:T(8,128)(2,1)S(1)} %get-tuple-element.49.after), channel_id=1, source_target_pairs={{0,128},{128,0},{1,129},{129,1},{2,130},{130,2},{3,131},{131,3},{4... | collective-permute-start | bytes 393224 | tf_op jit(solution)/shard_map/ppermute | solution.py:32
  95.7 5.2 %collective-permute-start.30 = (bf16[2,128,256]{2,1,0:T(8,128)(2,1)S(1)}, bf16[2,128,256]{2,1,0:T(8,128)(2,1)S(1)}, u32[]{:S(2)}, u32[]{:S(2)}) collective-permute-start(bf16[2,128,256]{2,1,0:T(8,128)(2,1)S(1)} %get-tuple-element.59), channel_id=1, source_target_pairs={{0,128},{128,0},{1,129},{129,1},{2,130},{130,2},{3,131},{131,3},{4... | collective-permute-start | bytes 393224 | tf_op jit(solution)/shard_map/ppermute | solution.py:32
  101.7 5.3 %collective-permute-done.26.theirs = bf16[2,128,256]{2,1,0:T(8,128)(2,1)S(1)} collective-permute-done((bf16[2,128,256]{2,1,0:T(8,128)(2,1)S(1)}, bf16[2,128,256]{2,1,0:T(8,128)(2,1)S(1)}, u32[]{:S(2)}, u32[]{:S(2)}) %collective-permute-start.26) | collective-permute-done | bytes 131104 | tf_op jit(solution)/shard_map/ppermute | solution.py:32
  107.7 3.2 %collective-permute-start.34 = (bf16[2,128,256]{2,1,0:T(8,128)(2,1)S(1)}, bf16[2,128,256]{2,1,0:T(8,128)(2,1)S(1)}, u32[]{:S(2)}, u32[]{:S(2)}) collective-permute-start(bf16[2,128,256]{2,1,0:T(8,128)(2,1)S(1)} %shard_map.96.after.lat1.refs_4_), channel_id=1, source_target_pairs={{0,32},{32,0},{64,96},{96,64},{1,33},{33,1},{65,97},{97,65},{2,34}... | collective-permute-start | bytes 393224 | tf_op jit(solution)/shard_map/ppermute | solution.py:32
  110.9 2.3 %collective-permute-start.35 = (bf16[2,128,256]{2,1,0:T(8,128)(2,1)S(1)}, bf16[2,128,256]{2,1,0:T(8,128)(2,1)S(1)}, u32[]{:S(2)}, u32[]{:S(2)}) collective-permute-start(bf16[2,128,256]{2,1,0:T(8,128)(2,1)S(1)} %shard_map.96.after.lat1.refs_4_), channel_id=1, source_target_pairs={{0,64},{32,96},{64,0},{96,32},{1,65},{33,97},{65,1},{97,33},{2,66}... | collective-permute-start | bytes 393224 | tf_op jit(solution)/shard_map/ppermute | solution.py:32
  113.1 2.4 %collective-permute-start.31 = (bf16[2,128,256]{2,1,0:T(8,128)(2,1)S(1)}, bf16[2,128,256]{2,1,0:T(8,128)(2,1)S(1)}, u32[]{:S(2)}, u32[]{:S(2)}) collective-permute-start(bf16[2,128,256]{2,1,0:T(8,128)(2,1)S(1)} %shard_map.94.after.lat0.refs_0_), channel_id=1, source_target_pairs={{0,32},{32,0},{64,96},{96,64},{1,33},{33,1},{65,97},{97,65},{2,34}... | collective-permute-start | bytes 393224 | tf_op jit(solution)/shard_map/ppermute | solution.py:32
  121.7 2.7 %collective-permute-start.38 = (bf16[2,128,256]{2,1,0:T(8,128)(2,1)S(1)}, bf16[2,128,256]{2,1,0:T(8,128)(2,1)S(1)}, u32[]{:S(2)}, u32[]{:S(2)}) collective-permute-start(bf16[2,128,256]{2,1,0:T(8,128)(2,1)S(1)} %shard_map.98.lat2.after.l0), channel_id=1, source_target_pairs={{0,64},{32,96},{64,0},{96,32},{1,65},{33,97},{65,1},{97,33},{2,66}... | collective-permute-start | bytes 393224 | tf_op jit(solution)/shard_map/ppermute | solution.py:32
  134.4 3.9 %collective-permute-start.43 = (bf16[4,32,576]{2,1,0:T(8,128)(2,1)S(1)}, bf16[4,32,576]{2,1,0:T(8,128)(2,1)S(1)}, u32[]{:S(2)}, u32[]{:S(2)}) collective-permute-start(bf16[4,32,576]{2,1,0:T(8,128)(2,1)S(1)} %get-tuple-element.65), channel_id=1, source_target_pairs={{0,24},{8,16},{16,8},{24,0},{1,25},{9,17},{17,9},{25,1},{2,26},{10... | collective-permute-start | bytes 442376 | tf_op jit(solution)/shard_map/ppermute | solution.py:32
  138.3 2.4 %collective-permute-done.41.p1 = bf16[4,32,576]{2,1,0:T(8,128)(2,1)S(1)} collective-permute-done((bf16[4,32,576]{2,1,0:T(8,128)(2,1)S(1)}, bf16[4,32,576]{2,1,0:T(8,128)(2,1)S(1)}, u32[]{:S(2)}, u32[]{:S(2)}) %collective-permute-start.41) | collective-permute-done | bytes 147488 | tf_op jit(solution)/shard_map/ppermute | solution.py:32
  142.2 3.1 %collective-permute-done.43.p3 = bf16[4,32,576]{2,1,0:T(8,128)(2,1)S(1)} collective-permute-done((bf16[4,32,576]{2,1,0:T(8,128)(2,1)S(1)}, bf16[4,32,576]{2,1,0:T(8,128)(2,1)S(1)}, u32[]{:S(2)}, u32[]{:S(2)}) %collective-permute-start.43) | collective-permute-done | bytes 147488 | tf_op jit(solution)/shard_map/ppermute | solution.py:32
  145.6 3.4 %collective-permute-start.45 = (bf16[32,576]{1,0:T(8,128)(2,1)S(1)}, bf16[32,576]{1,0:T(8,128)(2,1)S(1)}, u32[]{:S(2)}, u32[]{:S(2)}) collective-permute-start(bf16[32,576]{1,0:T(8,128)(2,1)S(1)} %get-tuple-element.68), channel_id=1, source_target_pairs={{0,4},{2,6},{4,0},{6,2},{1,5},{3,7},{5,1},{7,3},{8,12},{10,14},{12... | collective-permute-start | bytes 110600 | tf_op jit(solution)/shard_map/ppermute | solution.py:32
  151.4 3.3 %collective-permute-done.46 = bf16[32,576]{1,0:T(8,128)(2,1)S(1)} collective-permute-done((bf16[32,576]{1,0:T(8,128)(2,1)S(1)}, bf16[32,576]{1,0:T(8,128)(2,1)S(1)}, u32[]{:S(2)}, u32[]{:S(2)}) %collective-permute-start.46) | collective-permute-done | bytes 36896 | tf_op jit(solution)/shard_map/ppermute | solution.py:32
  (127 shorter events, 67.2 us)
Async XLA Ops:
  0.6 10.1 %collective-permute-start = (bf16[144,128]{1,0:T(8,128)(2,1)}, bf16[144,128]{1,0:T(8,128)(2,1)S(1)}, u32[]{:S(2)}, u32[]{:S(2)}) collective-permute-start(bf16[144,128]{1,0:T(8,128)(2,1)} %bitcast.21), channel_id=1, source_target_pairs={{0,16},{1,17},{2,18},{3,19},{4,60},{5,61},{6,62},{7,63},{8,72},{9,... | collective-permute-start | bytes 110600 | tf_op jit(solution)/shard_map/ppermute | solution.py:278
  18.7 9.4 %collective-permute-start.5 = (bf16[4,144,128]{2,1,0:T(8,128)(2,1)S(1)}, bf16[4,144,128]{2,1,0:T(8,128)(2,1)S(1)}, u32[]{:S(2)}, u32[]{:S(2)}) collective-permute-start(bf16[4,144,128]{2,1,0:T(8,128)(2,1)S(1)} %pad_maximum_fusion.1), channel_id=1, source_target_pairs={{0,16},{8,24},{16,0},{24,8},{1,17},{9,25},{17,1},{25,9},{2,18},{10... | collective-permute-start | bytes 442376 | tf_op jit(solution)/shard_map/ppermute | solution.py:32
  58.5 8.6 %collective-permute-start.16 = (bf16[4,32,576]{2,1,0:T(8,128)(2,1)S(1)}, bf16[4,32,576]{2,1,0:T(8,128)(2,1)S(1)}, u32[]{:S(2)}, u32[]{:S(2)}) collective-permute-start(bf16[4,32,576]{2,1,0:T(8,128)(2,1)S(1)} %pad_maximum_fusion), channel_id=1, source_target_pairs={{0,16},{8,24},{16,0},{24,8},{1,17},{9,25},{17,1},{25,9},{2,18},{10... | collective-permute-start | bytes 442376 | tf_op jit(solution)/shard_map/ppermute | solution.py:32
  72.7 8.3 %collective-permute-start.19 = (bf16[2,128,256]{2,1,0:T(8,128)(2,1)S(1)}, bf16[2,128,256]{2,1,0:T(8,128)(2,1)S(1)}, u32[]{:S(2)}, u32[]{:S(2)}) collective-permute-start(bf16[2,128,256]{2,1,0:T(8,128)(2,1)S(1)} %get-tuple-element.45), channel_id=1, source_target_pairs={{0,64},{32,96},{64,0},{96,32},{1,65},{33,97},{65,1},{97,33},{2,66}... | collective-permute-start | bytes 393224 | tf_op jit(solution)/shard_map/ppermute | solution.py:32
  74.1 10.0 %collective-permute-start.20 = (bf16[2,128,256]{2,1,0:T(8,128)(2,1)S(1)}, bf16[2,128,256]{2,1,0:T(8,128)(2,1)S(1)}, u32[]{:S(2)}, u32[]{:S(2)}) collective-permute-start(bf16[2,128,256]{2,1,0:T(8,128)(2,1)S(1)} %get-tuple-element.46), channel_id=1, source_target_pairs={{0,32},{32,0},{64,96},{96,64},{1,33},{33,1},{65,97},{97,65},{2,34}... | collective-permute-start | bytes 393224 | tf_op jit(solution)/shard_map/ppermute | solution.py:32
  75.3 10.3 %collective-permute-start.21 = (bf16[2,128,256]{2,1,0:T(8,128)(2,1)S(1)}, bf16[2,128,256]{2,1,0:T(8,128)(2,1)S(1)}, u32[]{:S(2)}, u32[]{:S(2)}) collective-permute-start(bf16[2,128,256]{2,1,0:T(8,128)(2,1)S(1)} %get-tuple-element.47), channel_id=1, source_target_pairs={{0,96},{32,64},{64,32},{96,0},{1,97},{33,65},{65,33},{97,1},{2,98}... | collective-permute-start | bytes 393224 | tf_op jit(solution)/shard_map/ppermute | solution.py:32
  78.4 8.3 %collective-permute-start.23 = (bf16[2,128,256]{2,1,0:T(8,128)(2,1)S(1)}, bf16[2,128,256]{2,1,0:T(8,128)(2,1)S(1)}, u32[]{:S(2)}, u32[]{:S(2)}) collective-permute-start(bf16[2,128,256]{2,1,0:T(8,128)(2,1)S(1)} %get-tuple-element.50), channel_id=1, source_target_pairs={{0,64},{32,96},{64,0},{96,32},{1,65},{33,97},{65,1},{97,33},{2,66}... | collective-permute-start | bytes 393224 | tf_op jit(solution)/shard_map/ppermute | solution.py:32
  79.8 8.6 %collective-permute-start.24 = (bf16[2,128,256]{2,1,0:T(8,128)(2,1)S(1)}, bf16[2,128,256]{2,1,0:T(8,128)(2,1)S(1)}, u32[]{:S(2)}, u32[]{:S(2)}) collective-permute-start(bf16[2,128,256]{2,1,0:T(8,128)(2,1)S(1)} %get-tuple-element.51), channel_id=1, source_target_pairs={{0,32},{32,0},{64,96},{96,64},{1,33},{33,1},{65,97},{97,65},{2,34}... | collective-permute-start | bytes 393224 | tf_op jit(solution)/shard_map/ppermute | solution.py:32
  81.0 13.1 %collective-permute-start.25 = (bf16[2,128,256]{2,1,0:T(8,128)(2,1)S(1)}, bf16[2,128,256]{2,1,0:T(8,128)(2,1)S(1)}, u32[]{:S(2)}, u32[]{:S(2)}) collective-permute-start(bf16[2,128,256]{2,1,0:T(8,128)(2,1)S(1)} %get-tuple-element.52), channel_id=1, source_target_pairs={{0,96},{32,64},{64,32},{96,0},{1,97},{33,65},{65,33},{97,1},{2,98}... | collective-permute-start | bytes 393224 | tf_op jit(solution)/shard_map/ppermute | solution.py:32
  84.1 11.5 %collective-permute-start.27 = (bf16[2,128,256]{2,1,0:T(8,128)(2,1)S(1)}, bf16[2,128,256]{2,1,0:T(8,128)(2,1)S(1)}, u32[]{:S(2)}, u32[]{:S(2)}) collective-permute-start(bf16[2,128,256]{2,1,0:T(8,128)(2,1)S(1)} %get-tuple-element.55), channel_id=1, source_target_pairs={{0,64},{32,96},{64,0},{96,32},{1,65},{33,97},{65,1},{97,33},{2,66}... | collective-permute-start | bytes 393224 | tf_op jit(solution)/shard_map/ppermute | solution.py:32
  85.6 10.1 %collective-permute-start.28 = (bf16[2,128,256]{2,1,0:T(8,128)(2,1)S(1)}, bf16[2,128,256]{2,1,0:T(8,128)(2,1)S(1)}, u32[]{:S(2)}, u32[]{:S(2)}) collective-permute-start(bf16[2,128,256]{2,1,0:T(8,128)(2,1)S(1)} %get-tuple-element.56), channel_id=1, source_target_pairs={{0,32},{32,0},{64,96},{96,64},{1,33},{33,1},{65,97},{97,65},{2,34}... | collective-permute-start | bytes 393224 | tf_op jit(solution)/shard_map/ppermute | solution.py:32
  86.7 9.0 %collective-permute-start.29 = (bf16[2,128,256]{2,1,0:T(8,128)(2,1)S(1)}, bf16[2,128,256]{2,1,0:T(8,128)(2,1)S(1)}, u32[]{:S(2)}, u32[]{:S(2)}) collective-permute-start(bf16[2,128,256]{2,1,0:T(8,128)(2,1)S(1)} %get-tuple-element.57), channel_id=1, source_target_pairs={{0,96},{32,64},{64,32},{96,0},{1,97},{33,65},{65,33},{97,1},{2,98}... | collective-permute-start | bytes 393224 | tf_op jit(solution)/shard_map/ppermute | solution.py:32
  88.4 12.7 %collective-permute-start.22 = (bf16[2,128,256]{2,1,0:T(8,128)(2,1)S(1)}, bf16[2,128,256]{2,1,0:T(8,128)(2,1)S(1)}, u32[]{:S(2)}, u32[]{:S(2)}) collective-permute-start(bf16[2,128,256]{2,1,0:T(8,128)(2,1)S(1)} %get-tuple-element.49.after), channel_id=1, source_target_pairs={{0,128},{128,0},{1,129},{129,1},{2,130},{130,2},{3,131},{131,3},{4... | collective-permute-start | bytes 393224 | tf_op jit(solution)/shard_map/ppermute | solution.py:32
  94.1 12.9 %collective-permute-start.26 = (bf16[2,128,256]{2,1,0:T(8,128)(2,1)S(1)}, bf16[2,128,256]{2,1,0:T(8,128)(2,1)S(1)}, u32[]{:S(2)}, u32[]{:S(2)}) collective-permute-start(bf16[2,128,256]{2,1,0:T(8,128)(2,1)S(1)} %get-tuple-element.54.after), channel_id=1, source_target_pairs={{0,128},{128,0},{1,129},{129,1},{2,130},{130,2},{3,131},{131,3},{4... | collective-permute-start | bytes 393224 | tf_op jit(solution)/shard_map/ppermute | solution.py:32
  95.7 19.8 %collective-permute-start.30 = (bf16[2,128,256]{2,1,0:T(8,128)(2,1)S(1)}, bf16[2,128,256]{2,1,0:T(8,128)(2,1)S(1)}, u32[]{:S(2)}, u32[]{:S(2)}) collective-permute-start(bf16[2,128,256]{2,1,0:T(8,128)(2,1)S(1)} %get-tuple-element.59), channel_id=1, source_target_pairs={{0,128},{128,0},{1,129},{129,1},{2,130},{130,2},{3,131},{131,3},{4... | collective-permute-start | bytes 393224 | tf_op jit(solution)/shard_map/ppermute | solution.py:32
  107.7 8.9 %collective-permute-start.34 = (bf16[2,128,256]{2,1,0:T(8,128)(2,1)S(1)}, bf16[2,128,256]{2,1,0:T(8,128)(2,1)S(1)}, u32[]{:S(2)}, u32[]{:S(2)}) collective-permute-start(bf16[2,128,256]{2,1,0:T(8,128)(2,1)S(1)} %shard_map.96.after.lat1.refs_4_), channel_id=1, source_target_pairs={{0,32},{32,0},{64,96},{96,64},{1,33},{33,1},{65,97},{97,65},{2,34}... | collective-permute-start | bytes 393224 | tf_op jit(solution)/shard_map/ppermute | solution.py:32
  110.9 9.2 %collective-permute-start.35 = (bf16[2,128,256]{2,1,0:T(8,128)(2,1)S(1)}, bf16[2,128,256]{2,1,0:T(8,128)(2,1)S(1)}, u32[]{:S(2)}, u32[]{:S(2)}) collective-permute-start(bf16[2,128,256]{2,1,0:T(8,128)(2,1)S(1)} %shard_map.96.after.lat1.refs_4_), channel_id=1, source_target_pairs={{0,64},{32,96},{64,0},{96,32},{1,65},{33,97},{65,1},{97,33},{2,66}... | collective-permute-start | bytes 393224 | tf_op jit(solution)/shard_map/ppermute | solution.py:32
  113.1 8.6 %collective-permute-start.36 = (bf16[2,128,256]{2,1,0:T(8,128)(2,1)S(1)}, bf16[2,128,256]{2,1,0:T(8,128)(2,1)S(1)}, u32[]{:S(2)}, u32[]{:S(2)}) collective-permute-start(bf16[2,128,256]{2,1,0:T(8,128)(2,1)S(1)} %shard_map.96.after.lat1.refs_4_), channel_id=1, source_target_pairs={{0,96},{32,64},{64,32},{96,0},{1,97},{33,65},{65,33},{97,1},{2,98}... | collective-permute-start | bytes 393224 | tf_op jit(solution)/shard_map/ppermute | solution.py:32
  113.1 11.3 %collective-permute-start.31 = (bf16[2,128,256]{2,1,0:T(8,128)(2,1)S(1)}, bf16[2,128,256]{2,1,0:T(8,128)(2,1)S(1)}, u32[]{:S(2)}, u32[]{:S(2)}) collective-permute-start(bf16[2,128,256]{2,1,0:T(8,128)(2,1)S(1)} %shard_map.94.after.lat0.refs_0_), channel_id=1, source_target_pairs={{0,32},{32,0},{64,96},{96,64},{1,33},{33,1},{65,97},{97,65},{2,34}... | collective-permute-start | bytes 393224 | tf_op jit(solution)/shard_map/ppermute | solution.py:32
  115.6 9.8 %collective-permute-start.32 = (bf16[2,128,256]{2,1,0:T(8,128)(2,1)S(1)}, bf16[2,128,256]{2,1,0:T(8,128)(2,1)S(1)}, u32[]{:S(2)}, u32[]{:S(2)}) collective-permute-start(bf16[2,128,256]{2,1,0:T(8,128)(2,1)S(1)} %shard_map.94.after.lat0.refs_0_), channel_id=1, source_target_pairs={{0,64},{32,96},{64,0},{96,32},{1,65},{33,97},{65,1},{97,33},{2,66}... | collective-permute-start | bytes 393224 | tf_op jit(solution)/shard_map/ppermute | solution.py:32
  116.6 10.0 %collective-permute-start.33 = (bf16[2,128,256]{2,1,0:T(8,128)(2,1)S(1)}, bf16[2,128,256]{2,1,0:T(8,128)(2,1)S(1)}, u32[]{:S(2)}, u32[]{:S(2)}) collective-permute-start(bf16[2,128,256]{2,1,0:T(8,128)(2,1)S(1)} %shard_map.94.after.lat0.refs_0_), channel_id=1, source_target_pairs={{0,96},{32,64},{64,32},{96,0},{1,97},{33,65},{65,33},{97,1},{2,98}... | collective-permute-start | bytes 393224 | tf_op jit(solution)/shard_map/ppermute | solution.py:32
  120.0 8.8 %collective-permute-start.37 = (bf16[2,128,256]{2,1,0:T(8,128)(2,1)S(1)}, bf16[2,128,256]{2,1,0:T(8,128)(2,1)S(1)}, u32[]{:S(2)}, u32[]{:S(2)}) collective-permute-start(bf16[2,128,256]{2,1,0:T(8,128)(2,1)S(1)} %shard_map.98.lat2.after.l0), channel_id=1, source_target_pairs={{0,32},{32,0},{64,96},{96,64},{1,33},{33,1},{65,97},{97,65},{2,34}... | collective-permute-start | bytes 393224 | tf_op jit(solution)/shard_map/ppermute | solution.py:32
  133.6 8.6 %collective-permute-start.42 = (bf16[4,32,576]{2,1,0:T(8,128)(2,1)S(1)}, bf16[4,32,576]{2,1,0:T(8,128)(2,1)S(1)}, u32[]{:S(2)}, u32[]{:S(2)}) collective-permute-start(bf16[4,32,576]{2,1,0:T(8,128)(2,1)S(1)} %get-tuple-element.64), channel_id=1, source_target_pairs={{0,16},{8,24},{16,0},{24,8},{1,17},{9,25},{17,1},{25,9},{2,18},{10... | collective-permute-start | bytes 442376 | tf_op jit(solution)/shard_map/ppermute | solution.py:32
  134.4 11.0 %collective-permute-start.43 = (bf16[4,32,576]{2,1,0:T(8,128)(2,1)S(1)}, bf16[4,32,576]{2,1,0:T(8,128)(2,1)S(1)}, u32[]{:S(2)}, u32[]{:S(2)}) collective-permute-start(bf16[4,32,576]{2,1,0:T(8,128)(2,1)S(1)} %get-tuple-element.65), channel_id=1, source_target_pairs={{0,24},{8,16},{16,8},{24,0},{1,25},{9,17},{17,9},{25,1},{2,26},{10... | collective-permute-start | bytes 442376 | tf_op jit(solution)/shard_map/ppermute | solution.py:32
  (28 other events, 280.6 us)
